TPU v7x, 32 devices: a whole 2x2x4 slice. The times are simulated.
32 devices in a mesh: ta: 4 (over y, x), gx: 2 (over core), gy: 4 (over z).
Axes of the slice: x: 2, y: 2, z: 4, core: 2. Of those that a mesh axis runs over, the one named last changes fastest.
Arguments:
- velocity: float32 [3, 4, 32, 64, 256], P(None, 'ta', 'gx', 'gy'), may hold values from -6 to 6
- pressure: float32 [4, 32, 64, 256], P('ta', 'gx', 'gy'), may hold values from -6 to 6
- forcing: float32 [3, 4, 32, 64, 256], P(None, 'ta', 'gx', 'gy'), may hold values from -6 to 6
- source: float32 [4, 32, 64, 256], P('ta', 'gx', 'gy'), may hold values from -6 to 6
- viscosity: float32 [3, 32, 64, 256], P(None, 'gx', 'gy'), may hold values from 0.05 to 0.5
Outputs:
- new_velocity: float32 [3, 4, 32, 64, 256], P(None, 'ta', 'gx', 'gy')
- new_pressure: float32 [4, 32, 64, 256], P('ta', 'gx', 'gy')
All inputs are finite; a program needn't handle non-finite values.
Results may differ from a plain program's by a relative error of at most 0.00002.
Values sent between devices are 32-bit elements; how exact they have to be, the bound alone decides.
A program may use at most 64 MiB of HBM per device.

v0:
```python
import jax
import jax.numpy as jnp
from jax import lax
from jax.sharding import PartitionSpec as P

inverse_step = 1.0
relax_factor = 1.5
damping = 0.8


def shifted(x, axis, by):
    length = lax.axis_size(axis)
    pairs = [(i, i + by) for i in range(length) if 0 <= i + by < length]
    return lax.ppermute(x, axis, pairs)


def extended(cells, sides, width):
    for axis, dim in sides:
        count = lax.axis_size(axis)
        head = lax.slice_in_dim(cells, 0, width, axis=dim)
        tail = lax.slice_in_dim(cells, cells.shape[dim] - width, cells.shape[dim], axis=dim)
        cells = jnp.concatenate(
            [
                lax.ppermute(tail, axis, [(i, (i + 1) % count) for i in range(count)]),
                cells,
                lax.ppermute(head, axis, [((i + 1) % count, i) for i in range(count)]),
            ],
            axis=dim,
        )
    return cells


def shifted_2(value, axis, steps):
    count = lax.axis_size(axis)
    pairs = [(source, (source + steps) % count) for source in range(count)]
    return lax.ppermute(value, axis, pairs)


def gradient(field):
    return jnp.stack(
        [
            jnp.roll(field, -1, -3) - field,
            jnp.roll(field, -1, -2) - field,
            jnp.roll(field, -1, -1) - field,
        ]
    )


def divergence(flux):
    return (
        flux[0]
        - jnp.roll(flux[0], 1, -3)
        + (flux[1] - jnp.roll(flux[1], 1, -2))
        + (flux[2] - jnp.roll(flux[2], 1, -1))
    )


def neighbours(field):
    total = jnp.roll(field, 1, -3) + jnp.roll(field, -1, -3)
    total = total + jnp.roll(field, 1, -2) + jnp.roll(field, -1, -2)
    return total + jnp.roll(field, 1, -1) + jnp.roll(field, -1, -1)


def diagonal_sum(coeff):
    return (
        coeff[0]
        + jnp.roll(coeff[0], 1, -3)
        + coeff[1]
        + jnp.roll(coeff[1], 1, -2)
        + coeff[2]
        + jnp.roll(coeff[2], 1, -1)
    )


def inner_part(field, margin):
    return field[..., margin : field.shape[-3] - margin, margin : field.shape[-2] - margin, :]


def split_fields(padded, slab_steps):
    first = 3 * slab_steps
    shape_rest = padded.shape[1:]
    flow = padded[:first].reshape((3, slab_steps) + shape_rest)
    press = padded[first : first + slab_steps]
    position = first + slab_steps
    drive = padded[position : position + first].reshape((3, slab_steps) + shape_rest)
    position = position + first
    source_pad = None
    visc = padded[position : position + 3][:, None]
    return (flow, press, drive, source_pad, visc)


def body(velocity, pressure, forcing, source, viscosity):
    slab_steps = velocity.shape[1]
    cells_x = velocity.shape[2]
    cells_y = velocity.shape[3]
    cells_z = velocity.shape[4]
    arrived = shifted(velocity[:, slab_steps - 1], "ta", 1)
    previous = jnp.concatenate([arrived[:, None], velocity[:, : slab_steps - 1]], axis=1)
    driven = forcing + inverse_step * previous
    flat_flow = velocity.reshape(3 * slab_steps, cells_x, cells_y, cells_z)
    flat_drive = driven.reshape(3 * slab_steps, cells_x, cells_y, cells_z)
    margin = 2
    stacked = jnp.concatenate([flat_flow, pressure, flat_drive, viscosity], axis=0)
    padded = extended(stacked, (("gx", 1), ("gy", 2)), margin)
    flow, press, drive, source_pad, visc = split_fields(padded, slab_steps)
    momentum = (
        drive - (inverse_step * flow + visc * (6.0 * flow - neighbours(flow))) - gradient(press)
    )
    coeff = 1.0 / (relax_factor * (inverse_step + 6.0 * visc))
    total = inner_part(diagonal_sum(coeff), margin)
    right = inner_part(divergence(coeff * momentum) + divergence(flow), margin) - source
    change = -damping * right / total
    coeff_inner = inner_part(coeff, 1)
    bordered = extended(change, (("gx", 1), ("gy", 2)), 1)
    applied = inner_part(divergence(coeff_inner * gradient(bordered)), 1)
    change = change - damping * (right - applied) / total
    upper_x = shifted_2(change[:, :1], "gx", -1)
    upper_y = shifted_2(change[:, :, :1], "gy", -1)
    step_x = jnp.concatenate([change[:, 1:], upper_x], axis=1) - change
    step_y = jnp.concatenate([change[:, :, 1:], upper_y], axis=2) - change
    step_z = jnp.roll(change, -1, -1) - change
    slopes = jnp.stack([step_x, step_y, step_z])
    correction = inner_part(coeff, margin) * (inner_part(momentum, margin) - slopes)
    return (velocity + correction, pressure + change)


def solution(mesh):
    placed = (
        P(None, "ta", "gx", "gy", None),
        P("ta", "gx", "gy", None),
        P(None, "ta", "gx", "gy", None),
        P("ta", "gx", "gy", None),
        P(None, "gx", "gy", None),
    )
    return jax.shard_map(
        body,
        mesh=mesh,
        in_specs=placed,
        out_specs=(P(None, "ta", "gx", "gy", None), P("ta", "gx", "gy", None)),
        check_vma=False,
    )
```

profile of v0, /device:TPU:4, one launch (start us, length us, event | category | flops | bytes accessed | tf_op | source)
XLA Modules:
  0.0 73.1 jit_solution(2722591697857891690)
XLA Ops:
  0.7 3.5 %collective-permute-start = (f32[3,16,16,256]{3,2,1,0:T(8,128)}, f32[3,16,16,256]{3,2,1,0:T(8,128)S(1)}, u32[]{:S(2)}, u32[]{:S(2)}) collective-permute-start(f32[3,16,16,256]{3,2,1,0:T(8,128)} %bitcast.81), channel_id=1, source_target_pairs={{0,8},{8,16},{16,24},{1,9},{9,17},{17,25},{2,10},{10,18},{18,26},{... | collective-permute-start | bytes 2359304 | tf_op jit(solution)/shard_map/ppermute | solution.py:14
  4.2 18.9 %collective-permute-done = f32[3,16,16,256]{3,2,1,0:T(8,128)S(1)} collective-permute-done((f32[3,16,16,256]{3,2,1,0:T(8,128)}, f32[3,16,16,256]{3,2,1,0:T(8,128)S(1)}, u32[]{:S(2)}, u32[]{:S(2)}) %collective-permute-start) | collective-permute-done | bytes 786464 | tf_op jit(solution)/shard_map/ppermute | solution.py:14
  23.1 1.3 %fusion.11 = f32[3,16,16,256]{3,2,1,0:T(8,128)S(1)} fusion(f32[3,16,16,256]{3,2,1,0:T(8,128)S(1)} %collective-permute-done, f32[3,1,16,16,256]{4,3,2,1,0:T(8,128)} %param.7), kind=kLoop, calls=%fused_computation.26 | loop fusion | flops 196608 | bytes 2359296 | tf_op jit(solution)/shard_map/reshape | solution.py:101
  24.5 0.5 collective-permute-start.2
  25.0 1.1 %collective-permute-done.1 = f32[10,2,16,256]{3,2,1,0:T(8,128)S(1)} collective-permute-done((f32[10,2,16,256]{3,2,1,0:T(8,128)S(1)}, f32[10,2,16,256]{3,2,1,0:T(8,128)S(1)}, u32[]{:S(2)}, u32[]{:S(2)}) %collective-permute-start.1) | collective-permute-done | bytes 327712 | tf_op jit(solution)/shard_map/ppermute | solution.py:24
  26.1 0.5 collective-permute-done.2
  26.6 0.3 pad_maximum_fusion.8
  26.9 1.6 %collective-permute-start.3 = (f32[10,20,2,256]{3,2,1,0:T(2,128)S(1)}, f32[10,20,2,256]{3,2,1,0:T(2,128)S(1)}, u32[]{:S(2)}, u32[]{:S(2)}) collective-permute-start(f32[10,20,2,256]{3,2,1,0:T(2,128)S(1)} %get-tuple-element.29), channel_id=1, source_target_pairs={{0,1},{1,2},{2,3},{3,0},{4,5},{5,6},{6,7},{7,4},{8,9},{9,10},{10,1... | collective-permute-start | bytes 1228808 | tf_op jit(solution)/shard_map/ppermute | solution.py:24
  28.5 2.2 %collective-permute-start.4 = (f32[10,20,2,256]{3,2,1,0:T(2,128)S(1)}, f32[10,20,2,256]{3,2,1,0:T(2,128)S(1)}, u32[]{:S(2)}, u32[]{:S(2)}) collective-permute-start(f32[10,20,2,256]{3,2,1,0:T(2,128)S(1)} %get-tuple-element.30), channel_id=1, source_target_pairs={{1,0},{2,1},{3,2},{0,3},{5,4},{6,5},{7,6},{4,7},{9,8},{10,9},{11,1... | collective-permute-start | bytes 1228808 | tf_op jit(solution)/shard_map/ppermute | solution.py:26
  30.8 10.4 %collective-permute-done.3 = f32[10,20,2,256]{3,2,1,0:T(2,128)S(1)} collective-permute-done((f32[10,20,2,256]{3,2,1,0:T(2,128)S(1)}, f32[10,20,2,256]{3,2,1,0:T(2,128)S(1)}, u32[]{:S(2)}, u32[]{:S(2)}) %collective-permute-start.3) | collective-permute-done | bytes 409632 | tf_op jit(solution)/shard_map/ppermute | solution.py:24
  41.1 7.4 %collective-permute-done.4 = f32[10,20,2,256]{3,2,1,0:T(2,128)S(1)} collective-permute-done((f32[10,20,2,256]{3,2,1,0:T(2,128)S(1)}, f32[10,20,2,256]{3,2,1,0:T(2,128)S(1)}, u32[]{:S(2)}, u32[]{:S(2)}) %collective-permute-start.4) | collective-permute-done | bytes 409632 | tf_op jit(solution)/shard_map/ppermute | solution.py:26
  48.5 1.2 %pad_maximum_fusion = f32[10,20,20,256]{3,2,1,0:T(8,128)S(1)} fusion(f32[10,20,2,256]{3,2,1,0:T(2,128)S(1)} %collective-permute-done.4, f32[10,2,16,256]{3,2,1,0:T(8,128)S(1)} %collective-permute-done.2, f32[3,16,16,256]{3,2,1,0:T(8,128)S(1)} %copy-done.1, f32[3,16,16,256]{3,2,1,0:T(8,128)S(1)} %fusion.11, f32[1,16,16,256]{3,2,1,0:T(8,128)S(1)} %copy-done.2, ...), kind=kLoop, calls=%fused_computation | loop fusion | flops 7168000 | bytes 8192000 | tf_op jit(solution)/shard_map/concatenate | solution.py:22
  50.3 0.3 fusion.31
  50.6 0.3 slice_bitcast_fusion.10
  51.1 0.5 slice_bitcast_fusion.1
  51.6 0.3 slice_bitcast_fusion.3
  52.0 0.3 fusion.37
  52.2 2.2 %fusion.30 = (f32[3,20,20,256]{3,2,1,0:T(8,128)S(1)}, f32[3,20,20,256]{3,2,1,0:T(8,128)S(1)}, f32[3,20,20,256]{3,2,1,0:T(8,128)S(1)}) fusion(f32[10,20,20,256]{3,2,1,0:T(8,128)S(1)} %pad_maximum_fusion, f32[1,20,20,256]{3,2,1,0:T(8,128)S(1)} %get-tuple-element.12, f32[1,20,20,256]{3,2,1,0:T(8,128)S(1)} %get-tuple-element.11, ...), kind=kLoop, calls=%fused_computation.106 | loop fusion | flops 7372800 | bytes 15974400 | tf_op jit(solution)/shard_map/mul | solution.py:111
  55.1 0.3 fusion.43
  55.5 0.6 copy-done.3
  56.0 0.9 %multiply_divide_fusion.1 = (f32[1,16,16,256]{3,2,1,0:T(8,128)S(1)}, f32[1,16,16,256]{3,2,1,0:T(8,128)S(1)}, f32[1,16,16,256]{3,2,1,0:T(8,128)S(1)}) fusion(f32[1,16,16,256]{3,2,1,0:T(8,128)S(1)} %copy-done.3, f32[1,20,20,255]{3,2,1,0:T(8,128)S(1)} %get-tuple-element.24, f32[1,20,20,1]{3,2,1,0:T(8,128)S(1)} %get-tuple-element.22, ...), kind=kLoop, calls=%fused_computation.98 | loop fusion | flops 1835008 | bytes 7094272 | tf_op jit(solution)/shard_map/div | solution.py:112
  57.1 0.5 collective-permute-start.6
  57.6 0.7 collective-permute-done.5
  58.5 1.2 %collective-permute-start.7 = (f32[1,18,1,256]{3,2,1,0:T(1,128)S(1)}, f32[1,18,1,256]{3,2,1,0:T(1,128)S(1)}, u32[]{:S(2)}, u32[]{:S(2)}) collective-permute-start(f32[1,18,1,256]{3,2,1,0:T(1,128)S(1)} %get-tuple-element.59), channel_id=1, source_target_pairs={{0,1},{1,2},{2,3},{3,0},{4,5},{5,6},{6,7},{7,4},{8,9},{9,10},{10,1... | collective-permute-start | bytes 55304 | tf_op jit(solution)/shard_map/ppermute | solution.py:24
  59.7 2.7 %collective-permute-start.8 = (f32[1,18,1,256]{3,2,1,0:T(1,128)S(1)}, f32[1,18,1,256]{3,2,1,0:T(1,128)S(1)}, u32[]{:S(2)}, u32[]{:S(2)}) collective-permute-start(f32[1,18,1,256]{3,2,1,0:T(1,128)S(1)} %get-tuple-element.60), channel_id=1, source_target_pairs={{1,0},{2,1},{3,2},{0,3},{5,4},{6,5},{7,6},{4,7},{9,8},{10,9},{11,1... | collective-permute-start | bytes 55304 | tf_op jit(solution)/shard_map/ppermute | solution.py:26
  62.4 1.7 %collective-permute-done.7 = f32[1,18,1,256]{3,2,1,0:T(1,128)S(1)} collective-permute-done((f32[1,18,1,256]{3,2,1,0:T(1,128)S(1)}, f32[1,18,1,256]{3,2,1,0:T(1,128)S(1)}, u32[]{:S(2)}, u32[]{:S(2)}) %collective-permute-start.7) | collective-permute-done | bytes 18464 | tf_op jit(solution)/shard_map/ppermute | solution.py:24
  64.5 0.2 maximum_subtract_fusion.3
  64.7 0.2 slice_multiply_fusion
  65.2 1.0 %fusion.32 = (f32[1,16,16,256]{3,2,1,0:T(8,128)}, f32[1,16,16,256]{3,2,1,0:T(8,128)S(1)}) fusion(f32[1,16,16,256]{3,2,1,0:T(8,128)S(1)} %copy-done.2, f32[1,16,16,256]{3,2,1,0:T(8,128)S(1)} %get-tuple-element.6, f32[1,16,16,256]{3,2,1,0:T(8,128)S(1)} %get-tuple-element.5, f32[1,18,18,255]{3,2,1,0:T(8,128)S(1)} %bitcast.85, f32[1,18,18,1]{3,2,1,0:T(8,128)S(1)} %slice.494, ...), kind=kLoop, calls=%fused_computation.108 | loop fusion | flops 983040 | bytes 3092480 | tf_op jit(solution)/shard_map/add | solution.py:124
  66.3 3.9 %collective-permute-start.10 = (f32[1,16,1,256]{3,2,1,0:T(1,128)S(1)}, f32[1,16,1,256]{3,2,1,0:T(1,128)S(1)}, u32[]{:S(2)}, u32[]{:S(2)}) collective-permute-start(f32[1,16,1,256]{3,2,1,0:T(1,128)S(1)} %slice.502), channel_id=1, source_target_pairs={{0,3},{1,0},{2,1},{3,2},{4,7},{5,4},{6,5},{7,6},{8,11},{9,8},{10,9... | collective-permute-start | bytes 49160 | tf_op jit(solution)/shard_map/ppermute | solution.py:36
  70.4 1.2 %collective-permute-done.10 = f32[1,16,1,256]{3,2,1,0:T(1,128)S(1)} collective-permute-done((f32[1,16,1,256]{3,2,1,0:T(1,128)S(1)}, f32[1,16,1,256]{3,2,1,0:T(1,128)S(1)}, u32[]{:S(2)}, u32[]{:S(2)}) %collective-permute-start.10) | collective-permute-done | bytes 16416 | tf_op jit(solution)/shard_map/ppermute | solution.py:36
  71.8 1.3 %fusion.10 = f32[3,1,16,16,256]{4,3,2,1,0:T(8,128)} fusion(f32[3,1,16,16,256]{4,3,2,1,0:T(8,128)S(1)} %copy-done, f32[3,1,20,20,256]{4,3,2,0,1:T(8,128)S(1)} %bitcast.86, f32[3,1,20,20,256]{4,3,2,1,0:T(8,128)S(1)} %get-tuple-element.26, f32[1,1,16,16,256]{4,3,2,1,0:T(8,128)S(1)} %get-tuple-element.62, f32[1,1,16,16,256]{4,3,2,1,0:T(8,128)S(1)} %get-tuple-element.63, ...), kind=kLoop, calls=%fused_computation.24 | loop fusion | flops 983040 | bytes 3932160 | tf_op jit(solution)/shard_map/add | solution.py:124
  (57 shorter events, 2.8 us)
Async XLA Ops:
  0.6 23.7 %copy-start = (f32[3,1,16,16,256]{4,3,2,1,0:T(8,128)S(1)}, f32[3,1,16,16,256]{4,3,2,1,0:T(8,128)}, u32[]{:S(2)}) copy-start(f32[3,1,16,16,256]{4,3,2,1,0:T(8,128)} %param.5) | copy-start | bytes 2359300
  0.6 23.7 %copy-start.2 = (f32[1,16,16,256]{3,2,1,0:T(8,128)S(1)}, f32[1,16,16,256]{3,2,1,0:T(8,128)}, u32[]{:S(2)}) copy-start(f32[1,16,16,256]{3,2,1,0:T(8,128)} %param.6) | copy-start | bytes 786436
  0.7 23.7 %copy-start.1 = (f32[3,16,16,256]{3,2,1,0:T(8,128)S(1)}, f32[3,16,16,256]{3,2,1,0:T(8,128)}, u32[]{:S(2)}) copy-start(f32[3,16,16,256]{3,2,1,0:T(8,128)} %param.9) | copy-start | bytes 2359300
  0.7 22.4 %collective-permute-start = (f32[3,16,16,256]{3,2,1,0:T(8,128)}, f32[3,16,16,256]{3,2,1,0:T(8,128)S(1)}, u32[]{:S(2)}, u32[]{:S(2)}) collective-permute-start(f32[3,16,16,256]{3,2,1,0:T(8,128)} %bitcast.81), channel_id=1, source_target_pairs={{0,8},{8,16},{16,24},{1,9},{9,17},{17,25},{2,10},{10,18},{18,26},{... | collective-permute-start | bytes 2359304 | tf_op jit(solution)/shard_map/ppermute | solution.py:14
  24.4 1.7 %collective-permute-start.1 = (f32[10,2,16,256]{3,2,1,0:T(8,128)S(1)}, f32[10,2,16,256]{3,2,1,0:T(8,128)S(1)}, u32[]{:S(2)}, u32[]{:S(2)}) collective-permute-start(f32[10,2,16,256]{3,2,1,0:T(8,128)S(1)} %get-tuple-element.31), channel_id=1, source_target_pairs={{0,4},{4,0},{1,5},{5,1},{2,6},{6,2},{3,7},{7,3},{8,12},{12,8},{9,1... | collective-permute-start | bytes 983048 | tf_op jit(solution)/shard_map/ppermute | solution.py:24
  24.5 2.1 %collective-permute-start.2 = (f32[10,2,16,256]{3,2,1,0:T(8,128)S(1)}, f32[10,2,16,256]{3,2,1,0:T(8,128)S(1)}, u32[]{:S(2)}, u32[]{:S(2)}) collective-permute-start(f32[10,2,16,256]{3,2,1,0:T(8,128)S(1)} %get-tuple-element.32), channel_id=1, source_target_pairs={{4,0},{0,4},{5,1},{1,5},{6,2},{2,6},{7,3},{3,7},{12,8},{8,12},{13,... | collective-permute-start | bytes 983048 | tf_op jit(solution)/shard_map/ppermute | solution.py:26
  26.9 14.2 %collective-permute-start.3 = (f32[10,20,2,256]{3,2,1,0:T(2,128)S(1)}, f32[10,20,2,256]{3,2,1,0:T(2,128)S(1)}, u32[]{:S(2)}, u32[]{:S(2)}) collective-permute-start(f32[10,20,2,256]{3,2,1,0:T(2,128)S(1)} %get-tuple-element.29), channel_id=1, source_target_pairs={{0,1},{1,2},{2,3},{3,0},{4,5},{5,6},{6,7},{7,4},{8,9},{9,10},{10,1... | collective-permute-start | bytes 1228808 | tf_op jit(solution)/shard_map/ppermute | solution.py:24
  28.5 20.0 %collective-permute-start.4 = (f32[10,20,2,256]{3,2,1,0:T(2,128)S(1)}, f32[10,20,2,256]{3,2,1,0:T(2,128)S(1)}, u32[]{:S(2)}, u32[]{:S(2)}) collective-permute-start(f32[10,20,2,256]{3,2,1,0:T(2,128)S(1)} %get-tuple-element.30), channel_id=1, source_target_pairs={{1,0},{2,1},{3,2},{0,3},{5,4},{6,5},{7,6},{4,7},{9,8},{10,9},{11,1... | collective-permute-start | bytes 1228808 | tf_op jit(solution)/shard_map/ppermute | solution.py:26
  55.1 1.0 %copy-start.3 = (f32[1,16,16,256]{3,2,1,0:T(8,128)S(1)}, f32[1,16,16,256]{3,2,1,0:T(8,128)}, u32[]{:S(2)}) copy-start(f32[1,16,16,256]{3,2,1,0:T(8,128)} %param.8) | copy-start | bytes 786436
  57.0 1.2 %collective-permute-start.5 = (f32[1,1,16,256]{3,2,1,0:T(8,128)S(1)}, f32[1,1,16,256]{3,2,1,0:T(8,128)S(1)}, u32[]{:S(2)}, u32[]{:S(2)}) collective-permute-start(f32[1,1,16,256]{3,2,1,0:T(8,128)S(1)} %get-tuple-element.64), channel_id=1, source_target_pairs={{0,4},{4,0},{1,5},{5,1},{2,6},{6,2},{3,7},{7,3},{8,12},{12,8},{9,1... | collective-permute-start | bytes 49160 | tf_op jit(solution)/shard_map/ppermute | solution.py:24
  57.1 1.3 %collective-permute-start.6 = (f32[1,1,16,256]{3,2,1,0:T(8,128)S(1)}, f32[1,1,16,256]{3,2,1,0:T(8,128)S(1)}, u32[]{:S(2)}, u32[]{:S(2)}) collective-permute-start(f32[1,1,16,256]{3,2,1,0:T(8,128)S(1)} %get-tuple-element.65), channel_id=1, source_target_pairs={{4,0},{0,4},{5,1},{1,5},{6,2},{2,6},{7,3},{3,7},{12,8},{8,12},{13,... | collective-permute-start | bytes 49160 | tf_op jit(solution)/shard_map/ppermute | solution.py:26
  58.5 5.6 %collective-permute-start.7 = (f32[1,18,1,256]{3,2,1,0:T(1,128)S(1)}, f32[1,18,1,256]{3,2,1,0:T(1,128)S(1)}, u32[]{:S(2)}, u32[]{:S(2)}) collective-permute-start(f32[1,18,1,256]{3,2,1,0:T(1,128)S(1)} %get-tuple-element.59), channel_id=1, source_target_pairs={{0,1},{1,2},{2,3},{3,0},{4,5},{5,6},{6,7},{7,4},{8,9},{9,10},{10,1... | collective-permute-start | bytes 55304 | tf_op jit(solution)/shard_map/ppermute | solution.py:24
  59.7 4.4 %collective-permute-start.8 = (f32[1,18,1,256]{3,2,1,0:T(1,128)S(1)}, f32[1,18,1,256]{3,2,1,0:T(1,128)S(1)}, u32[]{:S(2)}, u32[]{:S(2)}) collective-permute-start(f32[1,18,1,256]{3,2,1,0:T(1,128)S(1)} %get-tuple-element.60), channel_id=1, source_target_pairs={{1,0},{2,1},{3,2},{0,3},{5,4},{6,5},{7,6},{4,7},{9,8},{10,9},{11,1... | collective-permute-start | bytes 55304 | tf_op jit(solution)/shard_map/ppermute | solution.py:26
  66.3 4.2 %collective-permute-start.9 = (f32[1,1,16,256]{3,2,1,0:T(8,128)S(1)}, f32[1,1,16,256]{3,2,1,0:T(8,128)S(1)}, u32[]{:S(2)}, u32[]{:S(2)}) collective-permute-start(f32[1,1,16,256]{3,2,1,0:T(8,128)S(1)} %slice.500), channel_id=1, source_target_pairs={{0,4},{4,0},{1,5},{5,1},{2,6},{6,2},{3,7},{7,3},{8,12},{12,8},{9,1... | collective-permute-start | bytes 49160 | tf_op jit(solution)/shard_map/ppermute | solution.py:36
  66.3 5.3 %collective-permute-start.10 = (f32[1,16,1,256]{3,2,1,0:T(1,128)S(1)}, f32[1,16,1,256]{3,2,1,0:T(1,128)S(1)}, u32[]{:S(2)}, u32[]{:S(2)}) collective-permute-start(f32[1,16,1,256]{3,2,1,0:T(1,128)S(1)} %slice.502), channel_id=1, source_target_pairs={{0,3},{1,0},{2,1},{3,2},{4,7},{5,4},{6,5},{7,6},{8,11},{9,8},{10,9... | collective-permute-start | bytes 49160 | tf_op jit(solution)/shard_map/ppermute | solution.py:36
where the time goes:
time: 73.8 us; the launch traced here: 73.1 us
  waiting for transfers between devices  42 us (57%)
  starting transfers between devices  16.4 us (22%)
  other arithmetic  9.67 us (13%)
  local copies, waits for them, and re-layouts  3.9 us (5%)
  between operations  1.12 us (2%)
    ppermute x1, waiting for transfers between devices, shifted(): return lax.ppermute(x, axis, pairs)  18.9 us
    ppermute x4, waiting for transfers between devices, extended(): lax.ppermute(tail, axis, [(i, (i + 1) % count) for i in range(count)])  13.9 us
    ppermute x4, waiting for transfers between devices, extended(): lax.ppermute(head, axis, [((i + 1) % count, i) for i in range(count)])  8.04 us
    ppermute x4, starting transfers between devices, extended(): lax.ppermute(head, axis, [((i + 1) % count, i) for i in range(count)])  5.94 us
    ppermute x2, starting transfers between devices, shifted_2(): return lax.ppermute(value, axis, pairs)  3.94 us
    ppermute x1, starting transfers between devices, shifted(): return lax.ppermute(x, axis, pairs)  3.53 us
    ppermute x4, starting transfers between devices, extended(): lax.ppermute(tail, axis, [(i, (i + 1) % count) for i in range(count)])  2.95 us
    add x2, other arithmetic, body(): return (velocity + correction, pressure + change)  2.29 us
  transfers between devices with their start and end apart: 11, of which 9 were waited for; matrix products, arithmetic and copies ran while one was open for 0% of the time, Pallas kernels for 0%

commit v1 on v0

v1 whole, which is shorter than its diff:
```python
import functools

import jax
import jax.numpy as jnp
from jax import lax
from jax.experimental import pallas as pl
from jax.experimental.pallas import tpu as pltpu
from jax.sharding import PartitionSpec as P

relax_factor = 1.5
damping = 0.8
MESH = pl.DeviceIdType.MESH


def loop(lo, hi, body):
    def step(i, carry):
        body(i)
        return carry

    if hi > lo:
        lax.fori_loop(lo, hi, step, 0, unroll=2 if (hi - lo) % 2 == 0 else 1)


def row_index(f):
    return lax.broadcasted_iota(jnp.int32, f.shape, 0)


def y_next(f, row):
    n = f.shape[0]
    return jnp.where(row_index(f) == n - 1, row, pltpu.roll(f, n - 1, 0))


def y_last(f, row):
    return jnp.where(row_index(f) == 0, row, pltpu.roll(f, 1, 0))


def z_next(f):
    return pltpu.roll(f, f.shape[1] - 1, 1)


def z_last(f):
    return pltpu.roll(f, 1, 1)


def groups_of(lo, hi, size):
    return [(a, min(a + size, hi)) for a in range(lo, hi, size)]


def kernel(
    slabs, nx_parts, ny_parts, groups,
    vel, prs, frc, src, vis, out_v, out_p,
    V, Pr, F, S, Nu, C, W, SC, c1, c2, OV, OP,
    sE, rE, sI, rI, yu_s, yd_s, yu_r, yd_r, Ch, f_s, f_r,
    c1d_s, c1u_s, c1d_r, c1u_r, c2x_s, c2y_s, c2y_r,
    load_sem, out_sem, send_sem, recv_sem,
):
    _, nx, ny, nz = vel.shape
    parts = (ny - 4) // 4
    ta, gx, gy = lax.axis_index("ta"), lax.axis_index("gx"), lax.axis_index("gy")
    t_next, t_prev = lax.rem(ta + 1, slabs), lax.rem(ta + slabs - 1, slabs)
    has_next, has_prev = ta < slabs - 1, ta > 0
    xu, xd = lax.rem(gx + 1, nx_parts), lax.rem(gx + nx_parts - 1, nx_parts)
    yu, yd = lax.rem(gy + 1, ny_parts), lax.rem(gy + ny_parts - 1, ny_parts)

    loads = [
        pltpu.make_async_copy(vel, V.at[:, pl.ds(1, nx)], load_sem.at[0]),
        pltpu.make_async_copy(vis, Nu.at[:, pl.ds(1, nx)], load_sem.at[1]),
        pltpu.make_async_copy(prs, Pr.at[pl.ds(0, nx)], load_sem.at[2]),
        pltpu.make_async_copy(frc, F, load_sem.at[3]),
        pltpu.make_async_copy(src, S, load_sem.at[4]),
    ]
    for copy in loads:
        copy.start()

    barrier = pltpu.get_barrier_semaphore()
    for axis, index in (("gx", xu), ("gx", xd), ("gy", yu), ("gy", yd)):
        pl.semaphore_signal(barrier, inc=1, device_id={axis: index}, device_id_type=MESH)

    @pl.when(has_next)
    def _():
        pl.semaphore_signal(barrier, inc=1, device_id={"ta": t_next}, device_id_type=MESH)

    @pl.when(has_prev)
    def _():
        pl.semaphore_signal(barrier, inc=1, device_id={"ta": t_prev}, device_id_type=MESH)

    def remote(k, source, target, axis, index):
        return pltpu.make_async_remote_copy(
            src_ref=source, dst_ref=target, send_sem=send_sem.at[k], recv_sem=recv_sem.at[k],
            device_id={axis: index}, device_id_type=MESH,
        )

    vx_up = remote(0, V.at[:, nx], V.at[:, 0], "gx", xu)
    vx_dn = remote(1, V.at[:, 1], V.at[:, nx + 1], "gx", xd)
    px_dn = remote(2, Pr.at[0], Pr.at[nx], "gx", xd)
    nx_up = remote(3, Nu.at[0, nx], Nu.at[0, 0], "gx", xu)
    ry_up = remote(4, yu_s, yu_r, "gy", yu)
    ry_dn = remote(5, yd_s, yd_r, "gy", yd)
    fx_up = remote(6, W.at[0, nx], W.at[0, 0], "gx", xu)
    fy_up = remote(7, f_s, f_r, "gy", yu)
    cx_dn = remote(8, c1.at[1], c1.at[nx + 1], "gx", xd)
    cx_up = remote(9, c1.at[nx], c1.at[0], "gx", xu)
    cy_dn = remote(10, c1d_s, c1d_r, "gy", yd)
    cy_up = remote(11, c1u_s, c1u_r, "gy", yu)
    ex_dn = remote(12, c2x_s, c2.at[nx], "gx", xd)
    ey_dn = remote(13, c2y_s, c2y_r, "gy", yd)
    edge = remote(14, sE, rE, "ta", t_next)
    pieces = [
        remote(15 + k, sI.at[pl.ds(a, b - a)], rI.at[pl.ds(a, b - a)], "ta", t_next)
        for k, (a, b) in enumerate(groups)
    ]

    loads[0].wait()
    loads[1].wait()
    loads[2].wait()

    def pack_edges(x):
        for c in range(3):
            sE[c, x, 0:2] = V[c, x + 1, 0:2]
            sE[c, x, 2:4] = V[c, x + 1, ny - 2 : ny]
            yu_s[c, x] = V[c, x + 1, ny - 1 : ny]
            yd_s[c, x] = V[c, x + 1, 0:1]
        yu_s[3, x] = Nu[1, x + 1, ny - 1 : ny]
        yd_s[3, x] = Pr[x, 0:1]

    def pack_inner(x):
        for c in range(3):
            for p in range(parts):
                sI[x, p, c] = V[c, x + 1, 2 + 4 * p : 6 + 4 * p]

    loop(0, nx, pack_edges)
    pl.semaphore_wait(barrier, 4 + has_next.astype(jnp.int32) + has_prev.astype(jnp.int32))

    @pl.when(has_next)
    def _():
        edge.start()

    for copy in (ry_up, ry_dn, vx_up, vx_dn, px_dn, nx_up):
        copy.start()

    loop(0, nx, pack_inner)

    @pl.when(has_next)
    def _():
        for copy in pieces:
            copy.start()

    def coeff_of(nu):
        return 1.0 / (relax_factor * (1.0 + 6.0 * nu))

    loads[3].wait()
    loads[4].wait()
    for copy in (vx_up, vx_dn, px_dn, nx_up, ry_up, ry_dn):
        copy.wait_recv()
    C[0, 0] = coeff_of(Nu[0, 0])

    def prepare(x):
        e = x + 1
        below = coeff_of(yu_r[3, x])
        Ch[x] = below
        coeff = [coeff_of(Nu[c, e]) for c in range(3)]
        for c in range(3):
            C[c, e] = coeff[c]
        total = coeff[0] + C[0, x] + coeff[1] + y_last(coeff[1], below) + coeff[2] + z_last(coeff[2])
        SC[x] = damping / total
        press = Pr[x]
        grads = (Pr[x + 1] - press, y_next(press, yd_r[3, x]) - press, z_next(press) - press)
        for c in range(3):
            v = V[c, e]
            near = V[c, e - 1] + V[c, e + 1] + y_last(v, yu_r[c, x]) + y_next(v, yd_r[c, x])
            near = near + z_last(v) + z_next(v)
            momentum = F[c, x] - (v + Nu[c, e] * (6.0 * v - near)) - grads[c]
            W[c, e] = v + coeff[c] * momentum

    loop(0, nx, prepare)

    def add_edges(x):
        for c in range(3):
            for s, t in ((0, 0), (2, ny - 2)):
                W[c, x + 1, t : t + 2] = (
                    W[c, x + 1, t : t + 2] + C[c, x + 1, t : t + 2] * rE[c, x, s : s + 2]
                )

    def add_inner(x):
        for c in range(3):
            for p in range(parts):
                t = 2 + 4 * p
                W[c, x + 1, t : t + 4] = W[c, x + 1, t : t + 4] + C[c, x + 1, t : t + 4] * rI[x, p, c]

    def arrive(k):
        @pl.when(has_prev)
        def _():
            pieces[k].wait_recv()
            loop(*groups[k], add_inner)

    @pl.when(has_prev)
    def _():
        edge.wait_recv()
        loop(0, nx, add_edges)

    def pack_flux(x):
        f_s[x] = W[1, x + 1, ny - 1 : ny]

    loop(0, nx, pack_flux)
    fy_up.start()
    arrive(0)
    arrive(1)
    fx_up.start()
    fx_up.wait_recv()
    fy_up.wait_recv()

    def sweep_one(x):
        e = x + 1
        w1, w2 = W[1, e], W[2, e]
        div = (W[0, e] - W[0, x]) + (w1 - y_last(w1, f_r[x])) + (w2 - z_last(w2))
        return SC[x] * (S[x] - div)

    def first_edges(x):
        change = sweep_one(x)
        c1[x + 1] = change
        c1d_s[x] = change[0:1]
        c1u_s[x] = change[ny - 1 : ny]

    loop(0, nx, first_edges)
    for copy in (cy_dn, cy_up, cx_dn, cx_up):
        copy.start()
    for copy in (cx_dn, cx_up, cy_dn, cy_up):
        copy.wait_recv()

    def sweep_two(x):
        e = x + 1
        here = c1[e]
        w0 = W[0, e] - C[0, e] * (c1[e + 1] - here)
        w0_last = W[0, x] - C[0, x] * (here - c1[x])
        w1 = W[1, e] - C[1, e] * (y_next(here, c1d_r[x]) - here)
        row = f_r[x] - Ch[x] * (here[0:1] - c1u_r[x])
        w2 = W[2, e] - C[2, e] * (z_next(here) - here)
        div = (w0 - w0_last) + (w1 - y_last(w1, row)) + (w2 - z_last(w2))
        return here + SC[x] * (S[x] - div)

    c2x_s[...] = sweep_two(0)

    def second_edges(x):
        c2y_s[x] = sweep_two(x)[0:1]

    loop(0, nx, second_edges)
    ey_dn.start()
    ex_dn.start()

    for copy in (cx_dn, cx_up):
        copy.wait_send()

    def first(x):
        c1[x + 1] = sweep_one(x)

    def second(x):
        c2[x] = sweep_two(x)

    done = 0
    for k in range(2, len(groups)):
        arrive(k)
        stop = groups[k][1] if k < len(groups) - 1 else nx
        loop(done, stop, first)
        loop(max(done - 1, 0), stop - 1 if stop < nx else nx, second)
        done = stop

    ex_dn.wait_recv()
    ey_dn.wait_recv()

    def finish(x):
        e = x + 1
        here = c2[x]
        OP[x] = Pr[x] + here
        OV[0, x] = W[0, e] - C[0, e] * (c2[x + 1] - here)
        OV[1, x] = W[1, e] - C[1, e] * (y_next(here, c2y_r[x]) - here)
        OV[2, x] = W[2, e] - C[2, e] * (z_next(here) - here)

    stores = []
    for k, (a, b) in enumerate(groups_of(0, nx, -(-nx // 4))):
        loop(a, b, finish)
        part = pl.ds(a, b - a)
        stores.append(pltpu.make_async_copy(OV.at[:, part], out_v.at[:, part], out_sem.at[2 * k]))
        stores.append(pltpu.make_async_copy(OP.at[part], out_p.at[part], out_sem.at[2 * k + 1]))
        for copy in stores[-2:]:
            copy.start()

    @pl.when(has_next)
    def _():
        edge.wait_send()
        for copy in pieces:
            copy.wait_send()

    for copy in (vx_up, vx_dn, px_dn, nx_up, ry_up, ry_dn, fx_up, fy_up, cy_dn, cy_up, ex_dn, ey_dn):
        copy.wait_send()
    for copy in stores:
        copy.wait()


def body(counts, velocity, pressure, forcing, source, viscosity):
    _, steps, nx, ny, nz = velocity.shape
    assert steps == 1 and nx >= 5 and ny >= 8 and ny % 4 == 0
    groups = [(0, 2), (nx - 2, nx)] + groups_of(2, nx - 2, 4)
    parts = (ny - 4) // 4
    vmem = lambda *shape: pltpu.VMEM(shape, jnp.float32)
    rows = lambda *lead: vmem(*lead, nx, 1, nz)
    any_space = pl.BlockSpec(memory_space=pl.ANY)
    out_v, out_p = pl.pallas_call(
        functools.partial(kernel, *counts, groups),
        out_shape=(
            jax.ShapeDtypeStruct((3, nx, ny, nz), jnp.float32),
            jax.ShapeDtypeStruct((nx, ny, nz), jnp.float32),
        ),
        in_specs=[any_space] * 5,
        out_specs=(any_space, any_space),
        scratch_shapes=[
            vmem(3, nx + 2, ny, nz), vmem(nx + 1, ny, nz), vmem(3, nx, ny, nz), vmem(nx, ny, nz),
            vmem(3, nx + 1, ny, nz), vmem(3, nx + 1, ny, nz), vmem(3, nx + 1, ny, nz),
            vmem(nx, ny, nz), vmem(nx + 2, ny, nz), vmem(nx + 1, ny, nz),
            vmem(3, nx, ny, nz), vmem(nx, ny, nz),
            vmem(3, nx, 4, nz), vmem(3, nx, 4, nz),
            vmem(nx, parts, 3, 4, nz), vmem(nx, parts, 3, 4, nz),
            rows(4), rows(4), rows(4), rows(4), rows(), rows(), rows(),
            rows(), rows(), rows(), rows(), vmem(ny, nz), rows(), rows(),
            pltpu.SemaphoreType.DMA((5,)),
            pltpu.SemaphoreType.DMA((8,)),
            pltpu.SemaphoreType.DMA((15 + len(groups),)),
            pltpu.SemaphoreType.DMA((15 + len(groups),)),
        ],
        compiler_params=pltpu.CompilerParams(
            collective_id=0, has_side_effects=True, vmem_limit_bytes=48 << 20
        ),
        name="smoother",
    )(velocity[:, 0], pressure[0], forcing[:, 0], source[0], viscosity)
    return out_v[:, None], out_p[None]


def solution(mesh):
    placed = (
        P(None, "ta", "gx", "gy", None),
        P("ta", "gx", "gy", None),
        P(None, "ta", "gx", "gy", None),
        P("ta", "gx", "gy", None),
        P(None, "gx", "gy", None),
    )
    counts = tuple(mesh.shape[axis] for axis in ("ta", "gx", "gy"))
    return jax.shard_map(
        functools.partial(body, counts),
        mesh=mesh,
        in_specs=placed,
        out_specs=(P(None, "ta", "gx", "gy", None), P("ta", "gx", "gy", None)),
        check_vma=False,
    )
```

time: 73.8 us -> 33.7 us (0.46)
  waiting for transfers between devices: 42 us -> 0 us
  Pallas kernels: 0 us -> 25.8 us
  starting transfers between devices: 16.4 us -> 0 us
  other arithmetic: 9.67 us -> 0 us
  local copies, waits for them, and re-layouts: 3.9 us -> 6.87 us
    ppermute x11 -> x0, waiting for transfers between devices: 42 us -> none  [the longest x1 18.9 us: shifted(): return lax.ppermute(x, axis, pairs)]
    pallas_call x0 -> x1, Pallas kernels: none -> 25.8 us  [body(): pl.pallas_call(functools.partial(kernel, *counts, groups), out_shape=(jax...]
    ppermute x11 -> x0, starting transfers between devices: 16.4 us -> none  [the longest x4 5.94 us: extended(): lax.ppermute(head, axis, [((i + 1) % count, i) for i in range(count)])]
    unnamed x8 -> x12, local copies, waits for them, and re-layouts: 0.59 us -> 6.87 us
    mul x2 -> x0, other arithmetic: 2.43 us -> none  [the longest x1 2.23 us: body(): coeff * momentum]
    add x2 -> x0, other arithmetic: 2.29 us -> none  [body(): return (velocity + correction, pressure + change)]
    slice x32 -> x0, local copies, waits for them, and re-layouts: 1.71 us -> none  [the longest x5 0.58 us: divergence(): jnp.roll(flux[2], 1, -1)]
    concatenate x9 -> x0, local copies, waits for them, and re-layouts: 1.51 us -> none  [the longest x2 0.73 us: neighbours(): return total + jnp.roll(field, 1, -1) + jnp.roll(field, -1, -1)]
  transfers between devices with their start and end apart: 11 -> 0, of which waited for: 9 -> 0; matrix products, arithmetic and copies ran while one was open for 0% -> 0% of each run, Pallas kernels for 0% -> 0%
where the time goes in v1:
time: 33.7 us; the launch traced here: 33.3 us
  Pallas kernels  25.8 us (77%)
  local copies, waits for them, and re-layouts  6.87 us (20%)
  between operations  0.65 us (2%)
    pallas_call x1, Pallas kernels, body(): pl.pallas_call(functools.partial(kernel, *counts, groups), out_shape=(jax...  25.8 us
    unnamed x12, local copies, waits for them, and re-layouts  6.87 us

profile of v1, /device:TPU:4, one launch (start us, length us, event | category | flops | bytes accessed | tf_op | source)
XLA Modules:
  0.0 33.3 jit_solution(11390337407723788195)
XLA Ops:
  0.6 0.0 copy-start
  0.6 1.1 %copy-done = f32[3,1,16,16,256]{4,3,2,1,0:T(8,128)S(1)} copy-done((f32[3,1,16,16,256]{4,3,2,1,0:T(8,128)S(1)}, f32[3,1,16,16,256]{4,3,2,1,0:T(8,128)}, u32[]{:S(2)}) %copy-start) | copy-done | bytes 786456
  1.8 0.0 copy-start.1
  1.8 1.1 %copy-done.1 = f32[3,1,16,16,256]{4,3,2,1,0:T(8,128)S(1)} copy-done((f32[3,1,16,16,256]{4,3,2,1,0:T(8,128)S(1)}, f32[3,1,16,16,256]{4,3,2,1,0:T(8,128)}, u32[]{:S(2)}) %copy-start.1) | copy-done | bytes 786456
  2.9 0.0 copy-start.2
  2.9 1.1 %copy-done.2 = f32[3,16,16,256]{3,2,1,0:T(8,128)S(1)} copy-done((f32[3,16,16,256]{3,2,1,0:T(8,128)S(1)}, f32[3,16,16,256]{3,2,1,0:T(8,128)}, u32[]{:S(2)}) %copy-start.2) | copy-done | bytes 786456
  4.0 0.0 copy-start.3
  4.0 0.9 %copy-done.3 = f32[1,16,16,256]{3,2,1,0:T(8,128)S(1)} copy-done((f32[1,16,16,256]{3,2,1,0:T(8,128)S(1)}, f32[1,16,16,256]{3,2,1,0:T(8,128)}, u32[]{:S(2)}) %copy-start.3) | copy-done | bytes 262168
  5.0 0.0 copy-start.4
  5.0 0.9 %copy-done.4 = f32[1,16,16,256]{3,2,1,0:T(8,128)S(1)} copy-done((f32[1,16,16,256]{3,2,1,0:T(8,128)S(1)}, f32[1,16,16,256]{3,2,1,0:T(8,128)}, u32[]{:S(2)}) %copy-start.4) | copy-done | bytes 262168
  5.9 25.8 %smoother.1 = (f32[3,16,16,256]{3,2,1,0:T(8,128)S(1)}, f32[16,16,256]{2,1,0:T(8,128)S(1)}) custom-call(f32[3,16,16,256]{3,2,1,0:T(8,128)S(1)} %bitcast.9, f32[16,16,256]{2,1,0:T(8,128)S(1)} %bitcast.12, f32[3,16,16,256]{3,2,1,0:T(8,128)S(1)} %bitcast.10, f32[16,16,256]{2,1,0:T(8,128)S(1)} %bitcast.13, f32[3,16,16,256]{3,2,1,0:T(8,128)S(1)} %copy-done.2), custom_call_target="tpu_custom_call" | custom-call | tf_op jit(solution)/shard_map/smoother/pallas_call | solution.py:307
  31.8 0.9 %copy.10 = f32[3,1,16,16,256]{4,3,2,1,0:T(8,128)} copy(f32[3,1,16,16,256]{4,3,2,1,0:T(8,128)S(1)} %bitcast.8) | data formatting | bytes 1572864
  32.6 0.7 %copy.11 = f32[1,16,16,256]{3,2,1,0:T(8,128)} copy(f32[1,16,16,256]{3,2,1,0:T(8,128)S(1)} %bitcast.11) | data formatting | bytes 524288
Async XLA Ops:
  0.6 1.1 %copy-start = (f32[3,1,16,16,256]{4,3,2,1,0:T(8,128)S(1)}, f32[3,1,16,16,256]{4,3,2,1,0:T(8,128)}, u32[]{:S(2)}) copy-start(f32[3,1,16,16,256]{4,3,2,1,0:T(8,128)} %param.5) | copy-start | bytes 2359300
  1.8 1.1 %copy-start.1 = (f32[3,1,16,16,256]{4,3,2,1,0:T(8,128)S(1)}, f32[3,1,16,16,256]{4,3,2,1,0:T(8,128)}, u32[]{:S(2)}) copy-start(f32[3,1,16,16,256]{4,3,2,1,0:T(8,128)} %param.7) | copy-start | bytes 2359300
  2.9 1.1 %copy-start.2 = (f32[3,16,16,256]{3,2,1,0:T(8,128)S(1)}, f32[3,16,16,256]{3,2,1,0:T(8,128)}, u32[]{:S(2)}) copy-start(f32[3,16,16,256]{3,2,1,0:T(8,128)} %vis.1) | copy-start | bytes 2359300
  4.0 0.9 %copy-start.3 = (f32[1,16,16,256]{3,2,1,0:T(8,128)S(1)}, f32[1,16,16,256]{3,2,1,0:T(8,128)}, u32[]{:S(2)}) copy-start(f32[1,16,16,256]{3,2,1,0:T(8,128)} %param.6) | copy-start | bytes 786436
  5.0 0.9 %copy-start.4 = (f32[1,16,16,256]{3,2,1,0:T(8,128)S(1)}, f32[1,16,16,256]{3,2,1,0:T(8,128)}, u32[]{:S(2)}) copy-start(f32[1,16,16,256]{3,2,1,0:T(8,128)} %param.8) | copy-start | bytes 786436

commit v2 on v1

--- a/solution.py
+++ b/solution.py
@@ -18,7 +18,7 @@
         return carry
 
     if hi > lo:
-        lax.fori_loop(lo, hi, step, 0, unroll=2 if (hi - lo) % 2 == 0 else 1)
+        lax.fori_loop(lo, hi, step, 0, unroll=hi - lo)
 
 
 def row_index(f):
@@ -50,7 +50,7 @@
     slabs, nx_parts, ny_parts, groups,
     vel, prs, frc, src, vis, out_v, out_p,
     V, Pr, F, S, Nu, C, W, SC, c1, c2, OV, OP,
-    sE, rE, sI, rI, yu_s, yd_s, yu_r, yd_r, Ch, f_s, f_r,
+    sE, rE, sI, rI, yu_s, yd_s, yu_r, yd_r, Ch, f_s, f_r, Fh, rP,
     c1d_s, c1u_s, c1d_r, c1u_r, c2x_s, c2y_s, c2y_r,
     load_sem, out_sem, send_sem, recv_sem,
 ):
@@ -105,19 +105,19 @@
     ex_dn = remote(12, c2x_s, c2.at[nx], "gx", xd)
     ey_dn = remote(13, c2y_s, c2y_r, "gy", yd)
     edge = remote(14, sE, rE, "ta", t_next)
+    border = remote(15, yu_r.at[1], rP, "ta", t_next)
     pieces = [
-        remote(15 + k, sI.at[pl.ds(a, b - a)], rI.at[pl.ds(a, b - a)], "ta", t_next)
+        remote(16 + k, sI.at[pl.ds(a, b - a)], rI.at[pl.ds(a, b - a)], "ta", t_next)
         for k, (a, b) in enumerate(groups)
     ]
 
-    loads[0].wait()
-    loads[1].wait()
-    loads[2].wait()
-
     def pack_edges(x):
         for c in range(3):
             sE[c, x, 0:2] = V[c, x + 1, 0:2]
             sE[c, x, 2:4] = V[c, x + 1, ny - 2 : ny]
+
+    def pack_rows(x):
+        for c in range(3):
             yu_s[c, x] = V[c, x + 1, ny - 1 : ny]
             yd_s[c, x] = V[c, x + 1, 0:1]
         yu_s[3, x] = Nu[1, x + 1, ny - 1 : ny]
@@ -128,6 +128,7 @@
             for p in range(parts):
                 sI[x, p, c] = V[c, x + 1, 2 + 4 * p : 6 + 4 * p]
 
+    loads[0].wait()
     loop(0, nx, pack_edges)
     pl.semaphore_wait(barrier, 4 + has_next.astype(jnp.int32) + has_prev.astype(jnp.int32))
 
@@ -135,6 +136,9 @@
     def _():
         edge.start()
 
+    loads[1].wait()
+    loads[2].wait()
+    loop(0, nx, pack_rows)
     for copy in (ry_up, ry_dn, vx_up, vx_dn, px_dn, nx_up):
         copy.start()
 
@@ -142,7 +146,14 @@
 
     @pl.when(has_next)
     def _():
-        for copy in pieces:
+        for copy in pieces[:2]:
+            copy.start()
+
+    ry_up.wait_recv()
+
+    @pl.when(has_next)
+    def _():
+        for copy in (border, *pieces[2:]):
             copy.start()
 
     def coeff_of(nu):
@@ -150,7 +161,7 @@
 
     loads[3].wait()
     loads[4].wait()
-    for copy in (vx_up, vx_dn, px_dn, nx_up, ry_up, ry_dn):
+    for copy in (vx_up, vx_dn, px_dn, nx_up, ry_dn):
         copy.wait_recv()
     C[0, 0] = coeff_of(Nu[0, 0])
 
@@ -171,8 +182,10 @@
             near = near + z_last(v) + z_next(v)
             momentum = F[c, x] - (v + Nu[c, e] * (6.0 * v - near)) - grads[c]
             W[c, e] = v + coeff[c] * momentum
+        f_s[x] = W[1, e, ny - 1 : ny]
 
     loop(0, nx, prepare)
+    fy_up.start()
 
     def add_edges(x):
         for c in range(3):
@@ -198,21 +211,26 @@
         edge.wait_recv()
         loop(0, nx, add_edges)
 
-    def pack_flux(x):
-        f_s[x] = W[1, x + 1, ny - 1 : ny]
-
-    loop(0, nx, pack_flux)
-    fy_up.start()
     arrive(0)
     arrive(1)
     fx_up.start()
+    fy_up.wait_recv()
+
+    @pl.when(has_prev)
+    def _():
+        border.wait_recv()
+        Fh[...] = f_r[...] + Ch[...] * rP[...]
+
+    @pl.when(jnp.logical_not(has_prev))
+    def _():
+        Fh[...] = f_r[...]
+
     fx_up.wait_recv()
-    fy_up.wait_recv()
 
     def sweep_one(x):
         e = x + 1
         w1, w2 = W[1, e], W[2, e]
-        div = (W[0, e] - W[0, x]) + (w1 - y_last(w1, f_r[x])) + (w2 - z_last(w2))
+        div = (W[0, e] - W[0, x]) + (w1 - y_last(w1, Fh[x])) + (w2 - z_last(w2))
         return SC[x] * (S[x] - div)
 
     def first_edges(x):
@@ -233,7 +251,7 @@
         w0 = W[0, e] - C[0, e] * (c1[e + 1] - here)
         w0_last = W[0, x] - C[0, x] * (here - c1[x])
         w1 = W[1, e] - C[1, e] * (y_next(here, c1d_r[x]) - here)
-        row = f_r[x] - Ch[x] * (here[0:1] - c1u_r[x])
+        row = Fh[x] - Ch[x] * (here[0:1] - c1u_r[x])
         w2 = W[2, e] - C[2, e] * (z_next(here) - here)
         div = (w0 - w0_last) + (w1 - y_last(w1, row)) + (w2 - z_last(w2))
         return here + SC[x] * (S[x] - div)
@@ -255,17 +273,6 @@
 
     def second(x):
         c2[x] = sweep_two(x)
-
-    done = 0
-    for k in range(2, len(groups)):
-        arrive(k)
-        stop = groups[k][1] if k < len(groups) - 1 else nx
-        loop(done, stop, first)
-        loop(max(done - 1, 0), stop - 1 if stop < nx else nx, second)
-        done = stop
-
-    ex_dn.wait_recv()
-    ey_dn.wait_recv()
 
     def finish(x):
         e = x + 1
@@ -276,17 +283,35 @@
         OV[2, x] = W[2, e] - C[2, e] * (z_next(here) - here)
 
     stores = []
-    for k, (a, b) in enumerate(groups_of(0, nx, -(-nx // 4))):
+
+    def emit(a, b):
+        k = len(stores)
         loop(a, b, finish)
         part = pl.ds(a, b - a)
-        stores.append(pltpu.make_async_copy(OV.at[:, part], out_v.at[:, part], out_sem.at[2 * k]))
-        stores.append(pltpu.make_async_copy(OP.at[part], out_p.at[part], out_sem.at[2 * k + 1]))
+        stores.append(pltpu.make_async_copy(OV.at[:, part], out_v.at[:, part], out_sem.at[k]))
+        stores.append(pltpu.make_async_copy(OP.at[part], out_p.at[part], out_sem.at[k + 1]))
         for copy in stores[-2:]:
             copy.start()
 
+    done = 0
+    for k in range(2, len(groups)):
+        last = k == len(groups) - 1
+        if last:
+            ex_dn.wait_recv()
+            ey_dn.wait_recv()
+            ready = done - 2
+            emit(0, ready)
+        arrive(k)
+        stop = nx if last else groups[k][1]
+        loop(done, stop, first)
+        loop(max(done - 1, 0), nx if last else stop - 1, second)
+        done = stop
+    emit(ready, nx)
+
     @pl.when(has_next)
     def _():
         edge.wait_send()
+        border.wait_send()
         for copy in pieces:
             copy.wait_send()
 
@@ -296,10 +321,20 @@
         copy.wait()
 
 
+def place(from_v, from_p, out_v, out_p, sem):
+    copies = [
+        pltpu.make_async_copy(from_v.at[c], out_v.at[c], sem.at[c]) for c in range(3)
+    ] + [pltpu.make_async_copy(from_p, out_p, sem.at[3])]
+    for copy in copies:
+        copy.start()
+    for copy in copies:
+        copy.wait()
+
+
 def body(counts, velocity, pressure, forcing, source, viscosity):
     _, steps, nx, ny, nz = velocity.shape
-    assert steps == 1 and nx >= 5 and ny >= 8 and ny % 4 == 0
-    groups = [(0, 2), (nx - 2, nx)] + groups_of(2, nx - 2, 4)
+    assert steps == 1 and nx >= 8 and ny >= 8 and ny % 4 == 0
+    groups = [(0, 2), (nx - 2, nx)] + groups_of(2, nx - 4, 5) + [(nx - 4, nx - 2)]
     parts = (ny - 4) // 4
     vmem = lambda *shape: pltpu.VMEM(shape, jnp.float32)
     rows = lambda *lead: vmem(*lead, nx, 1, nz)
@@ -319,18 +354,30 @@
             vmem(3, nx, ny, nz), vmem(nx, ny, nz),
             vmem(3, nx, 4, nz), vmem(3, nx, 4, nz),
             vmem(nx, parts, 3, 4, nz), vmem(nx, parts, 3, 4, nz),
-            rows(4), rows(4), rows(4), rows(4), rows(), rows(), rows(),
+            rows(4), rows(4), rows(4), rows(4), rows(), rows(), rows(), rows(), rows(),
             rows(), rows(), rows(), rows(), vmem(ny, nz), rows(), rows(),
             pltpu.SemaphoreType.DMA((5,)),
-            pltpu.SemaphoreType.DMA((8,)),
-            pltpu.SemaphoreType.DMA((15 + len(groups),)),
-            pltpu.SemaphoreType.DMA((15 + len(groups),)),
+            pltpu.SemaphoreType.DMA((4,)),
+            pltpu.SemaphoreType.DMA((16 + len(groups),)),
+            pltpu.SemaphoreType.DMA((16 + len(groups),)),
         ],
         compiler_params=pltpu.CompilerParams(
             collective_id=0, has_side_effects=True, vmem_limit_bytes=48 << 20
         ),
         name="smoother",
-    )(velocity[:, 0], pressure[0], forcing[:, 0], source[0], viscosity)
+    )(*(pltpu.with_memory_space_constraint(a, pltpu.HBM) for a in (velocity[:, 0], pressure[0], forcing[:, 0], source[0], viscosity)))
+    out_v, out_p = pl.pallas_call(
+        place,
+        out_shape=(
+            jax.ShapeDtypeStruct(out_v.shape, jnp.float32),
+            jax.ShapeDtypeStruct(out_p.shape, jnp.float32),
+        ),
+        in_specs=[any_space] * 2,
+        out_specs=(any_space, any_space),
+        scratch_shapes=[pltpu.SemaphoreType.DMA((4,))],
+        compiler_params=pltpu.CompilerParams(vmem_limit_bytes=1 << 20),
+        name="place",
+    )(out_v, out_p)
     return out_v[:, None], out_p[None]
 
 

time: 33.7 us -> 25.5 us (0.76)
  local copies, waits for them, and re-layouts: 6.87 us -> 0 us
  Pallas kernels: 25.8 us -> 24.7 us
    unnamed x12 -> x0, local copies, waits for them, and re-layouts: 6.87 us -> none
    pallas_call x1, Pallas kernels: 25.8 us -> 23.7 us  [body(): pl.pallas_call(functools.partial(kernel, *counts, groups), out_shape=(jax...]
    pallas_call x0 -> x1, Pallas kernels: none -> 1 us  [body(): pl.pallas_call(place, out_shape=(jax.ShapeDtypeStruct(out_v.shape, jnp.fl...]
where the time goes in v2:
time: 25.5 us; the launch traced here: 25.4 us
  Pallas kernels  24.7 us (97%)
  between operations  0.64 us (3%)
    pallas_call x1, Pallas kernels, body(): pl.pallas_call(functools.partial(kernel, *counts, groups), out_shape=(jax...  23.7 us
    pallas_call x1, Pallas kernels, body(): pl.pallas_call(place, out_shape=(jax.ShapeDtypeStruct(out_v.shape, jnp.fl...  1 us

profile of v2, /device:TPU:4, one launch (start us, length us, event | category | flops | bytes accessed | tf_op | source)
XLA Modules:
  0.0 25.4 jit_solution(11566982304664729879)
XLA Ops:
  0.6 23.7 %smoother.1 = (f32[3,16,16,256]{3,2,1,0:T(8,128)S(1)}, f32[16,16,256]{2,1,0:T(8,128)S(1)}) custom-call(f32[3,16,16,256]{3,2,1,0:T(8,128)} %bitcast.8, f32[16,16,256]{2,1,0:T(8,128)} %bitcast.10, f32[3,16,16,256]{3,2,1,0:T(8,128)} %bitcast.9, f32[16,16,256]{2,1,0:T(8,128)} %bitcast.11, f32[3,16,16,256]{3,2,1,0:T(8,128)} %vis.1), custom_call_target="tpu_custom_call" | custom-call | tf_op jit(solution)/shard_map/smoother/pallas_call | solution.py:342
  24.4 1.0 %place.1 = (f32[3,16,16,256]{3,2,1,0:T(8,128)}, f32[16,16,256]{2,1,0:T(8,128)}) custom-call(f32[3,16,16,256]{3,2,1,0:T(8,128)S(1)} %get-tuple-element.6.from_v, f32[16,16,256]{2,1,0:T(8,128)S(1)} %get-tuple-element.7.from_p), custom_call_target="tpu_custom_call" | custom-call | tf_op jit(solution)/shard_map/place/pallas_call | solution.py:369

commit v3 on v2

--- a/solution.py
+++ b/solution.py
@@ -49,10 +49,10 @@
 def kernel(
     slabs, nx_parts, ny_parts, groups,
     vel, prs, frc, src, vis, out_v, out_p,
-    V, Pr, F, S, Nu, C, W, SC, c1, c2, OV, OP,
-    sE, rE, sI, rI, yu_s, yd_s, yu_r, yd_r, Ch, f_s, f_r, Fh, rP,
+    V, Pr, F, S, Nu, C, W, SC, c1, c2,
+    sE, rE, sI, rI, yu_s, yd_s, yu_r, yd_r, Ch, f_s, f_r, Fh, rP, rX, fe_r,
     c1d_s, c1u_s, c1d_r, c1u_r, c2x_s, c2y_s, c2y_r,
-    load_sem, out_sem, send_sem, recv_sem,
+    load_sem, send_sem, recv_sem,
 ):
     _, nx, ny, nz = vel.shape
     parts = (ny - 4) // 4
@@ -104,10 +104,12 @@
     cy_up = remote(11, c1u_s, c1u_r, "gy", yu)
     ex_dn = remote(12, c2x_s, c2.at[nx], "gx", xd)
     ey_dn = remote(13, c2y_s, c2y_r, "gy", yd)
-    edge = remote(14, sE, rE, "ta", t_next)
+    edge = remote(14, sE.at[:, pl.ds(2, nx - 2)], rE.at[:, pl.ds(2, nx - 2)], "ta", t_next)
+    planes = remote(16, vel.at[:, pl.ds(0, 2)], rX, "ta", t_next)
+    fe_up = remote(17 + len(groups), W.at[0, nx], fe_r, "gx", xu)
     border = remote(15, yu_r.at[1], rP, "ta", t_next)
     pieces = [
-        remote(16 + k, sI.at[pl.ds(a, b - a)], rI.at[pl.ds(a, b - a)], "ta", t_next)
+        remote(17 + k, sI.at[pl.ds(a, b - a)], rI.at[pl.ds(a, b - a)], "ta", t_next)
         for k, (a, b) in enumerate(groups)
     ]
 
@@ -128,9 +130,14 @@
             for p in range(parts):
                 sI[x, p, c] = V[c, x + 1, 2 + 4 * p : 6 + 4 * p]
 
+    pl.semaphore_wait(barrier, 4 + has_next.astype(jnp.int32) + has_prev.astype(jnp.int32))
+
+    @pl.when(has_next)
+    def _():
+        planes.start()
+
     loads[0].wait()
-    loop(0, nx, pack_edges)
-    pl.semaphore_wait(barrier, 4 + has_next.astype(jnp.int32) + has_prev.astype(jnp.int32))
+    loop(2, nx, pack_edges)
 
     @pl.when(has_next)
     def _():
@@ -142,26 +149,32 @@
     for copy in (ry_up, ry_dn, vx_up, vx_dn, px_dn, nx_up):
         copy.start()
 
-    loop(0, nx, pack_inner)
-
-    @pl.when(has_next)
-    def _():
-        for copy in pieces[:2]:
-            copy.start()
-
-    ry_up.wait_recv()
-
-    @pl.when(has_next)
-    def _():
-        for copy in (border, *pieces[2:]):
-            copy.start()
-
     def coeff_of(nu):
         return 1.0 / (relax_factor * (1.0 + 6.0 * nu))
 
     loads[3].wait()
+    vx_up.wait_recv()
+    vx_dn.wait_recv()
+
+    def pack_flux(x):
+        e, j = x + 1, ny - 1
+        v, nu = V[1, e, j:ny], Nu[1, e, j:ny]
+        near = V[1, e - 1, j:ny] + V[1, e + 1, j:ny] + V[1, e, j - 1 : j] + z_last(v) + z_next(v)
+        momentum = F[1, x, j:ny] - (v + nu * (6.0 * v - near)) + Pr[x, j:ny]
+        f_s[x] = v + coeff_of(nu) * momentum
+
+    loop(0, nx, pack_flux)
+    fy_up.start()
+    loop(2, nx, pack_inner)
+    ry_up.wait_recv()
+
+    @pl.when(has_next)
+    def _():
+        for copy in (border, *pieces):
+            copy.start()
+
     loads[4].wait()
-    for copy in (vx_up, vx_dn, px_dn, nx_up, ry_dn):
+    for copy in (px_dn, nx_up, ry_dn):
         copy.wait_recv()
     C[0, 0] = coeff_of(Nu[0, 0])
 
@@ -182,10 +195,8 @@
             near = near + z_last(v) + z_next(v)
             momentum = F[c, x] - (v + Nu[c, e] * (6.0 * v - near)) - grads[c]
             W[c, e] = v + coeff[c] * momentum
-        f_s[x] = W[1, e, ny - 1 : ny]
 
     loop(0, nx, prepare)
-    fy_up.start()
 
     def add_edges(x):
         for c in range(3):
@@ -208,40 +219,54 @@
 
     @pl.when(has_prev)
     def _():
+        planes.wait_recv()
+        for c in range(3):
+            W[c, 1:3] = W[c, 1:3] + C[c, 1:3] * rX[c]
         edge.wait_recv()
-        loop(0, nx, add_edges)
-
-    arrive(0)
-    arrive(1)
-    fx_up.start()
+        loop(2, nx, add_edges)
+
+    fe_up.start()
     fy_up.wait_recv()
 
+    def close_flux(x):
+        Fh[x] = f_r[x] + Ch[x] * (yu_r[3, x] * V[1, x + 1, 0:1] - Pr[x, 0:1])
+
+    loop(0, nx, close_flux)
+
     @pl.when(has_prev)
     def _():
         border.wait_recv()
-        Fh[...] = f_r[...] + Ch[...] * rP[...]
-
-    @pl.when(jnp.logical_not(has_prev))
-    def _():
-        Fh[...] = f_r[...]
-
-    fx_up.wait_recv()
-
-    def sweep_one(x):
+        Fh[...] = Fh[...] + Ch[...] * rP[...]
+
+    fe_up.wait_recv()
+
+    def sweep_one(x, w0_last=None):
         e = x + 1
         w1, w2 = W[1, e], W[2, e]
-        div = (W[0, e] - W[0, x]) + (w1 - y_last(w1, Fh[x])) + (w2 - z_last(w2))
+        div = (W[0, e] - (W[0, x] if w0_last is None else w0_last)) + (w1 - y_last(w1, Fh[x])) + (w2 - z_last(w2))
         return SC[x] * (S[x] - div)
 
-    def first_edges(x):
-        change = sweep_one(x)
+    def first(x):
+        c1[x + 1] = sweep_one(x)
+
+    def first_edges(x, w0_last=None):
+        change = sweep_one(x, w0_last)
         c1[x + 1] = change
         c1d_s[x] = change[0:1]
         c1u_s[x] = change[ny - 1 : ny]
 
-    loop(0, nx, first_edges)
-    for copy in (cy_dn, cy_up, cx_dn, cx_up):
-        copy.start()
+    first_edges(0, fe_r[...])
+    loop(1, nx, first_edges)
+    cy_dn.start()
+    cy_up.start()
+    fe_up.wait_send()
+    arrive(0)
+    fx_up.start()
+    first(nx - 1)
+    cx_up.start()
+    fx_up.wait_recv()
+    first(0)
+    cx_dn.start()
     for copy in (cx_dn, cx_up, cy_dn, cy_up):
         copy.wait_recv()
 
@@ -268,33 +293,22 @@
     for copy in (cx_dn, cx_up):
         copy.wait_send()
 
-    def first(x):
-        c1[x + 1] = sweep_one(x)
-
     def second(x):
         c2[x] = sweep_two(x)
 
     def finish(x):
         e = x + 1
         here = c2[x]
-        OP[x] = Pr[x] + here
-        OV[0, x] = W[0, e] - C[0, e] * (c2[x + 1] - here)
-        OV[1, x] = W[1, e] - C[1, e] * (y_next(here, c2y_r[x]) - here)
-        OV[2, x] = W[2, e] - C[2, e] * (z_next(here) - here)
-
-    stores = []
+        out_p[x] = Pr[x] + here
+        out_v[0, x] = W[0, e] - C[0, e] * (c2[x + 1] - here)
+        out_v[1, x] = W[1, e] - C[1, e] * (y_next(here, c2y_r[x]) - here)
+        out_v[2, x] = W[2, e] - C[2, e] * (z_next(here) - here)
 
     def emit(a, b):
-        k = len(stores)
         loop(a, b, finish)
-        part = pl.ds(a, b - a)
-        stores.append(pltpu.make_async_copy(OV.at[:, part], out_v.at[:, part], out_sem.at[k]))
-        stores.append(pltpu.make_async_copy(OP.at[part], out_p.at[part], out_sem.at[k + 1]))
-        for copy in stores[-2:]:
-            copy.start()
 
     done = 0
-    for k in range(2, len(groups)):
+    for k in range(1, len(groups)):
         last = k == len(groups) - 1
         if last:
             ex_dn.wait_recv()
@@ -310,6 +324,7 @@
 
     @pl.when(has_next)
     def _():
+        planes.wait_send()
         edge.wait_send()
         border.wait_send()
         for copy in pieces:
@@ -317,8 +332,6 @@
 
     for copy in (vx_up, vx_dn, px_dn, nx_up, ry_up, ry_dn, fx_up, fy_up, cy_dn, cy_up, ex_dn, ey_dn):
         copy.wait_send()
-    for copy in stores:
-        copy.wait()
 
 
 def place(from_v, from_p, out_v, out_p, sem):
@@ -334,7 +347,7 @@
 def body(counts, velocity, pressure, forcing, source, viscosity):
     _, steps, nx, ny, nz = velocity.shape
     assert steps == 1 and nx >= 8 and ny >= 8 and ny % 4 == 0
-    groups = [(0, 2), (nx - 2, nx)] + groups_of(2, nx - 4, 5) + [(nx - 4, nx - 2)]
+    groups = [(nx - 2, nx)] + groups_of(2, nx - 4, 5) + [(nx - 4, nx - 2)]
     parts = (ny - 4) // 4
     vmem = lambda *shape: pltpu.VMEM(shape, jnp.float32)
     rows = lambda *lead: vmem(*lead, nx, 1, nz)
@@ -346,20 +359,18 @@
             jax.ShapeDtypeStruct((nx, ny, nz), jnp.float32),
         ),
         in_specs=[any_space] * 5,
-        out_specs=(any_space, any_space),
+        out_specs=(pl.BlockSpec(memory_space=pltpu.VMEM),) * 2,
         scratch_shapes=[
             vmem(3, nx + 2, ny, nz), vmem(nx + 1, ny, nz), vmem(3, nx, ny, nz), vmem(nx, ny, nz),
             vmem(3, nx + 1, ny, nz), vmem(3, nx + 1, ny, nz), vmem(3, nx + 1, ny, nz),
             vmem(nx, ny, nz), vmem(nx + 2, ny, nz), vmem(nx + 1, ny, nz),
-            vmem(3, nx, ny, nz), vmem(nx, ny, nz),
             vmem(3, nx, 4, nz), vmem(3, nx, 4, nz),
             vmem(nx, parts, 3, 4, nz), vmem(nx, parts, 3, 4, nz),
-            rows(4), rows(4), rows(4), rows(4), rows(), rows(), rows(), rows(), rows(),
+            rows(4), rows(4), rows(4), rows(4), rows(), rows(), rows(), rows(), rows(), vmem(3, 2, ny, nz), vmem(ny, nz),
             rows(), rows(), rows(), rows(), vmem(ny, nz), rows(), rows(),
             pltpu.SemaphoreType.DMA((5,)),
-            pltpu.SemaphoreType.DMA((4,)),
-            pltpu.SemaphoreType.DMA((16 + len(groups),)),
-            pltpu.SemaphoreType.DMA((16 + len(groups),)),
+            pltpu.SemaphoreType.DMA((18 + len(groups),)),
+            pltpu.SemaphoreType.DMA((18 + len(groups),)),
         ],
         compiler_params=pltpu.CompilerParams(
             collective_id=0, has_side_effects=True, vmem_limit_bytes=48 << 20

time: 25.5 us -> 25.5 us (level)
  no operation moved by 1% of the time
where the time goes in v3:
time: 25.5 us; the launch traced here: 25.4 us
  Pallas kernels  24.7 us (97%)
  between operations  0.64 us (3%)
    pallas_call x1, Pallas kernels, body(): pl.pallas_call(functools.partial(kernel, *counts, groups), out_shape=(jax...  23.7 us
    pallas_call x1, Pallas kernels, body(): pl.pallas_call(place, out_shape=(jax.ShapeDtypeStruct(out_v.shape, jnp.fl...  1 us

profile of v3, /device:TPU:4, one launch (start us, length us, event | category | flops | bytes accessed | tf_op | source)
XLA Modules:
  0.0 25.4 jit_solution(5930910692286483084)
XLA Ops:
  0.6 23.7 %smoother.1 = (f32[3,16,16,256]{3,2,1,0:T(8,128)S(1)}, f32[16,16,256]{2,1,0:T(8,128)S(1)}) custom-call(f32[3,16,16,256]{3,2,1,0:T(8,128)} %bitcast.8, f32[16,16,256]{2,1,0:T(8,128)} %bitcast.10, f32[3,16,16,256]{3,2,1,0:T(8,128)} %bitcast.9, f32[16,16,256]{2,1,0:T(8,128)} %bitcast.11, f32[3,16,16,256]{3,2,1,0:T(8,128)} %vis.1), custom_call_target="tpu_custom_call" | custom-call | tf_op jit(solution)/shard_map/smoother/pallas_call | solution.py:355
  24.4 1.0 %place.1 = (f32[3,16,16,256]{3,2,1,0:T(8,128)}, f32[16,16,256]{2,1,0:T(8,128)}) custom-call(f32[3,16,16,256]{3,2,1,0:T(8,128)S(1)} %get-tuple-element.6.from_v, f32[16,16,256]{2,1,0:T(8,128)S(1)} %get-tuple-element.7.from_p), custom_call_target="tpu_custom_call" | custom-call | tf_op jit(solution)/shard_map/place/pallas_call | solution.py:380
